TPU v7x, 32 devices: a whole 2x2x4 slice. The times are simulated.
32 devices in a mesh: section: 2 (over y), rows: 4 (over z), heads: 4 (over x, core).
Axes of the slice: x: 2, y: 2, z: 4, core: 2. Of those that a mesh axis runs over, the one named last changes fastest.
Arguments:
- tokens: bfloat16 [2, 2048, 4, 1024], P('section', 'heads', 'rows'), may hold values from -6 to 6
- image_lengths: int32 [2, 4, 6], P(None, 'rows'), may hold values from 64 to 576, as said below
- tile_ranks: int32 [2, 4, 6], P(None, 'rows'), may hold values from 0 to 5, each once within a row
- w_qkv: bfloat16 [1024, 3, 1024], P(None, None, 'heads'), may hold values from -0.1875 to 0.1875
- bias_qv: bfloat16 [2, 1024], P(None, 'heads'), may hold values from -3 to 3
- w_out: bfloat16 [1024, 1024], P('heads'), may hold values from -1.5 to 1.5
- bias_out: bfloat16 [1024], replicated, may hold values from -3 to 3
- w_up: bfloat16 [1024, 4096], P(None, 'heads'), may hold values from -0.1875 to 0.1875
- bias_up: bfloat16 [4096], P('heads'), may hold values from -3 to 3
- w_down: bfloat16 [4096, 1024], P('heads'), may hold values from -0.09375 to 0.09375
- bias_down: bfloat16 [1024], replicated, may hold values from -3 to 3
- ln1_gain: bfloat16 [1024], replicated, may hold values from 0.5 to 1.5
- ln1_bias: bfloat16 [1024], replicated, may hold values from -3 to 3
- ln2_gain: bfloat16 [1024], replicated, may hold values from 0.5 to 1.5
- ln2_bias: bfloat16 [1024], replicated, may hold values from -3 to 3
- grad_out: bfloat16 [2, 2048, 4, 1024], P(None, None, 'rows', ('section', 'heads')), may hold values from -6 to 6
- grad_tap: bfloat16 [2, 2048, 4, 1024], P(None, None, 'rows', ('section', 'heads')), may hold values from -6 to 6
Outputs:
- block_output: bfloat16 [2, 2048, 4, 1024], P(None, None, 'rows', ('section', 'heads'))
- input_tap: bfloat16 [2, 2048, 4, 1024], P(None, None, 'rows', ('section', 'heads'))
- grad_tokens: float32 [2, 2048, 4, 1024], P('section', 'heads', 'rows')
- grad_w_qkv: float32 [1024, 3, 1024], P(None, None, 'heads')
- grad_bias_qv: float32 [2, 1024], P(None, 'heads')
- grad_w_out: float32 [1024, 1024], P('heads')
- grad_bias_out: float32 [1024], replicated
- grad_w_up: float32 [1024, 4096], P(None, 'heads')
- grad_bias_up: float32 [4096], P('heads')
- grad_w_down: float32 [4096, 1024], P('heads')
- grad_bias_down: float32 [1024], replicated
- grad_ln1_gain: float32 [1024], replicated
- grad_ln1_bias: float32 [1024], replicated
- grad_ln2_gain: float32 [1024], replicated
- grad_ln2_bias: float32 [1024], replicated
Inputs may be any that keep to these rules, and one draw needn't show every extreme that they name: `image_lengths`: each row holds the patch counts of the 6 images of one sequence, in packing order, summing to 1920; the remaining positions of the 2048 are padding; every row has an image of exactly 576 patches and one of exactly 64. `tile_ranks`: each row is an ordering of the images 0 to 5: their places in the decoder's order.
All inputs are finite; a program needn't handle non-finite values.
Results may differ from a plain program's by a relative error of at most 0.024.
Values may be sent and summed in bfloat16 or wider, within the bound.
A program may use at most 192 MiB of HBM per device.

v0:
```python
from functools import partial
import jax
import jax.numpy as jnp
from jax import lax
from jax.sharding import PartitionSpec as P

HD = 64
EPSILON = 1e-06
MASKED = -1e30


def layer_norm(values_in, norm_gain, norm_shift):
    average = jnp.mean(values_in, axis=-1, keepdims=True)
    centred = values_in - average
    variance = jnp.mean(centred * centred, axis=-1, keepdims=True)
    return centred * lax.rsqrt(variance + EPSILON) * norm_gain + norm_shift


def gelu_exact(values_in):
    return jax.nn.gelu(values_in, approximate=False)


def image_tables(lengths, tile_order, extent):
    image_ends = jnp.cumsum(lengths)
    image_starts = image_ends - lengths
    earlier = (tile_order[None, :] < tile_order[:, None]).astype(jnp.int32)
    new_starts = jnp.sum(earlier * lengths[None, :], axis=1)
    position = jnp.arange(extent, dtype=jnp.int32)
    segment = jnp.sum((position[:, None] >= image_ends[None, :]).astype(jnp.int32), axis=1)
    inside_new = (position[:, None] >= new_starts[None, :]) & (
        position[:, None] < (new_starts + lengths)[None, :]
    )
    source = position + jnp.sum(jnp.where(inside_new, image_starts - new_starts, 0), axis=1)
    inside_old = segment[:, None] == jnp.arange(lengths.shape[0], dtype=jnp.int32)[None, :]
    target = position + jnp.sum(jnp.where(inside_old, new_starts - image_starts, 0), axis=1)
    return (segment, source, target)


def reorder_pair(first_rows, second_rows, picks):
    extent = picks.shape[-1]
    columns = jnp.arange(extent, dtype=jnp.int32)
    selector = (picks[..., None] == columns).astype(jnp.bfloat16)
    first_out = jnp.einsum(
        "hspq,hqsc->hpsc", selector, first_rows, preferred_element_type=jnp.float32
    )
    second_out = jnp.einsum(
        "hspq,hqsc->hpsc", selector, second_rows, preferred_element_type=jnp.float32
    )
    return (first_out.astype(jnp.bfloat16), second_out.astype(jnp.bfloat16))


def masked_scores(queries, key_seq, segment_rows, segment_seq):
    scores = jnp.einsum(
        "qhd,khd->hqk", queries, key_seq, preferred_element_type=jnp.float32
    ) * HD ** (-0.5)
    allowed = segment_rows[:, None] == segment_seq[None, :]
    return jnp.where(allowed[None], scores, MASKED)


def attend_forward(query_seq, key_seq, value_seq, segment_seq, block_rows):
    extent = query_seq.shape[0]
    block_count = extent // block_rows
    query_blocks = query_seq.reshape((block_count, block_rows) + query_seq.shape[1:])
    segment_blocks = segment_seq.reshape(block_count, block_rows)

    def one_block(block_item):
        queries, segment_rows = block_item
        scores = masked_scores(queries, key_seq, segment_rows, segment_seq)
        row_max = jnp.max(scores, axis=-1, keepdims=True)
        exponent = jnp.exp(scores - row_max)
        row_total = jnp.sum(exponent, axis=-1, keepdims=True)
        attend_prob = (exponent / row_total).astype(jnp.bfloat16)
        mixture = jnp.einsum(
            "hqk,khd->qhd", attend_prob, value_seq, preferred_element_type=jnp.float32
        )
        return (mixture, (row_max + jnp.log(row_total))[..., 0])

    mixture, log_sum = lax.map(one_block, (query_blocks, segment_blocks))
    return (mixture.reshape(query_seq.shape), log_sum)


def attend_backward(query_seq, key_seq, value_seq, segment_seq, log_sum, grad_seq, block_rows):
    extent = query_seq.shape[0]
    block_count = extent // block_rows
    query_blocks = query_seq.reshape((block_count, block_rows) + query_seq.shape[1:])
    grad_blocks = grad_seq.reshape((block_count, block_rows) + grad_seq.shape[1:])
    segment_blocks = segment_seq.reshape(block_count, block_rows)

    def one_block(running, block_item):
        key_acc, value_acc = running
        queries, segment_rows, log_rows, grad_rows = block_item
        scores = masked_scores(queries, key_seq, segment_rows, segment_seq)
        attend_prob = jnp.exp(scores - log_rows[..., None])
        prob_low = attend_prob.astype(jnp.bfloat16)
        grad_prob = jnp.einsum(
            "qhd,khd->hqk", grad_rows, value_seq, preferred_element_type=jnp.float32
        )
        inner = jnp.sum(attend_prob * grad_prob, axis=-1, keepdims=True)
        grad_score = (attend_prob * (grad_prob - inner) * HD ** (-0.5)).astype(jnp.bfloat16)
        grad_query = jnp.einsum(
            "hqk,khd->qhd", grad_score, key_seq, preferred_element_type=jnp.float32
        )
        key_acc = key_acc + jnp.einsum(
            "hqk,qhd->khd", grad_score, queries, preferred_element_type=jnp.float32
        )
        value_acc = value_acc + jnp.einsum(
            "hqk,qhd->khd", prob_low, grad_rows, preferred_element_type=jnp.float32
        )
        return ((key_acc, value_acc), grad_query)

    zero_rows = jnp.zeros(key_seq.shape, jnp.float32)
    (grad_key, grad_value), grad_query = lax.scan(
        one_block, (zero_rows, zero_rows), (query_blocks, segment_blocks, log_sum, grad_blocks)
    )
    return (grad_query.reshape(query_seq.shape), grad_key, grad_value)


def per_device(
    tokens,
    image_lengths,
    tile_ranks,
    w_qkv,
    bias_qv,
    w_out,
    bias_out,
    w_up,
    bias_up,
    w_down,
    bias_down,
    ln1_gain,
    ln1_bias,
    ln2_gain,
    ln2_bias,
    grad_out,
    grad_tap,
):
    own_tokens = tokens[0]
    part_rows = own_tokens.shape[0]
    seq_count = own_tokens.shape[1]
    full_len = part_rows * lax.axis_size("heads")
    block_rows = min(512, full_len)
    section_at = lax.axis_index("section")
    head_at = lax.axis_index("heads")
    halves = image_lengths.shape[0]
    image_count = image_lengths.shape[2]
    flat_lengths = image_lengths.reshape(halves * seq_count, image_count)
    flat_orders = tile_ranks.reshape(halves * seq_count, image_count)
    segments, sources, targets = jax.vmap(partial(image_tables, extent=full_len))(
        flat_lengths, flat_orders
    )
    segments = segments.reshape(halves, seq_count, full_len)
    sources = sources.reshape(halves, seq_count, full_len)
    targets = targets.reshape(halves, seq_count, full_len)
    own_segments = lax.dynamic_index_in_dim(segments, section_at, 0, keepdims=False)
    row_places = head_at * part_rows + jnp.arange(part_rows, dtype=jnp.int32)
    valid_rows = (
        (jnp.take(own_segments, row_places, axis=1) < image_count).astype(jnp.float32).T[:, :, None]
    )
    token_values = own_tokens.astype(jnp.float32)
    normed_one = layer_norm(token_values, ln1_gain, ln1_bias).astype(jnp.bfloat16)
    gathered_one = lax.all_gather(normed_one, "heads", axis=0, tiled=True)
    projected = jnp.einsum("rsd,dck->rsck", gathered_one, w_qkv, preferred_element_type=jnp.float32)
    query_all = (projected[:, :, 0] + bias_qv[0]).astype(jnp.bfloat16)
    key_all = projected[:, :, 1].astype(jnp.bfloat16)
    value_all = (projected[:, :, 2] + bias_qv[1]).astype(jnp.bfloat16)
    head_groups = query_all.shape[2] // HD
    split_shape = (full_len, seq_count, head_groups, HD)
    query_heads = query_all.reshape(split_shape)
    key_heads = key_all.reshape(split_shape)
    value_heads = value_all.reshape(split_shape)
    which = 0
    mixture, log_sum = attend_forward(
        query_heads[:, which],
        key_heads[:, which],
        value_heads[:, which],
        own_segments[which],
        block_rows,
    )
    mixtures = [mixture]
    log_sums = [log_sum]
    attended = (
        jnp.stack(mixtures, axis=1)
        .reshape(full_len, seq_count, head_groups * HD)
        .astype(jnp.bfloat16)
    )
    picked = attended
    attn_sum = (
        lax.psum_scatter(
            jnp.einsum("rsk,kd->rsd", picked, w_out, preferred_element_type=jnp.float32).astype(
                jnp.bfloat16
            ),
            "heads",
            scatter_dimension=0,
            tiled=True,
        ).astype(jnp.float32)
        + bias_out
    )
    after_attn = token_values + attn_sum
    normed_two = layer_norm(after_attn, ln2_gain, ln2_bias).astype(jnp.bfloat16)
    gathered_two = lax.all_gather(normed_two, "heads", axis=0, tiled=True)
    pre_act = (
        jnp.einsum("rsd,df->rsf", gathered_two, w_up, preferred_element_type=jnp.float32) + bias_up
    )
    activated = gelu_exact(pre_act).astype(jnp.bfloat16)
    picked = activated
    mlp_sum = (
        lax.psum_scatter(
            jnp.einsum("rsf,fd->rsd", picked, w_down, preferred_element_type=jnp.float32).astype(
                jnp.bfloat16
            ),
            "heads",
            scatter_dimension=0,
            tiled=True,
        ).astype(jnp.float32)
        + bias_down
    )
    block_out = ((after_attn + mlp_sum) * valid_rows).astype(jnp.bfloat16)
    sent_out, sent_tap = (
        lax.all_to_all(block_out, ("section", "heads"), split_axis=2, concat_axis=0, tiled=True),
        lax.all_to_all(own_tokens, ("section", "heads"), split_axis=2, concat_axis=0, tiled=True),
    )
    decoder_shape = (halves, full_len, seq_count, sent_out.shape[2])
    output_dec, tap_dec = reorder_pair(
        sent_out.reshape(decoder_shape), sent_tap.reshape(decoder_shape), sources
    )
    encoder_shape = (halves * full_len, seq_count, grad_out.shape[3])
    back_out, back_tap = reorder_pair(grad_out, grad_tap, targets)
    grad_block, grad_direct = (
        lax.all_to_all(
            back_out.reshape(encoder_shape),
            ("section", "heads"),
            split_axis=0,
            concat_axis=2,
            tiled=True,
        ),
        lax.all_to_all(
            back_tap.reshape(encoder_shape),
            ("section", "heads"),
            split_axis=0,
            concat_axis=2,
            tiled=True,
        ),
    )
    grad_mlp_full = grad_block.astype(jnp.float32) * valid_rows
    grad_mlp = grad_mlp_full.astype(jnp.bfloat16)
    grad_b_down = jnp.sum(grad_mlp, axis=(0, 1), dtype=jnp.float32)
    grad_mlp_all = lax.all_gather(grad_mlp, "heads", axis=0, tiled=True)
    grad_w_down_part = jnp.einsum(
        "rsf,rsd->fd", activated, grad_mlp_all, preferred_element_type=jnp.float32
    )
    grad_act = jnp.einsum("rsd,fd->rsf", grad_mlp_all, w_down, preferred_element_type=jnp.float32)
    gelu_back = jax.vjp(gelu_exact, pre_act)[1]
    grad_pre = gelu_back(grad_act)[0].astype(jnp.bfloat16)
    grad_w_up_part = jnp.einsum(
        "rsd,rsf->df", gathered_two, grad_pre, preferred_element_type=jnp.float32
    )
    grad_b_up = jnp.sum(grad_pre, axis=(0, 1), dtype=jnp.float32)
    picked = grad_pre
    grad_normed_two = lax.psum_scatter(
        jnp.einsum("rsf,df->rsd", picked, w_up, preferred_element_type=jnp.float32).astype(
            jnp.bfloat16
        ),
        "heads",
        scatter_dimension=0,
        tiled=True,
    ).astype(jnp.float32)
    norm_two_back = jax.vjp(layer_norm, after_attn, ln2_gain, ln2_bias)[1]
    grad_after, grad_gain_two, grad_shift_two = norm_two_back(grad_normed_two)
    grad_after = grad_after + grad_mlp_full
    grad_attn = grad_after.astype(jnp.bfloat16)
    grad_b_out = jnp.sum(grad_attn, axis=(0, 1), dtype=jnp.float32)
    grad_attn_all = lax.all_gather(grad_attn, "heads", axis=0, tiled=True)
    grad_w_out_part = jnp.einsum(
        "rsk,rsd->kd", attended, grad_attn_all, preferred_element_type=jnp.float32
    )
    grad_attended = (
        jnp.einsum("rsd,kd->rsk", grad_attn_all, w_out, preferred_element_type=jnp.float32)
        .astype(jnp.bfloat16)
        .reshape(split_shape)
    )
    which = 0
    grad_query, grad_key, grad_value = attend_backward(
        query_heads[:, which],
        key_heads[:, which],
        value_heads[:, which],
        own_segments[which],
        log_sums[which],
        grad_attended[:, which],
        block_rows,
    )
    query_grads = [grad_query]
    key_grads = [grad_key]
    value_grads = [grad_value]
    flat_shape = (full_len, seq_count, head_groups * HD)
    grad_query_all = jnp.stack(query_grads, axis=1).reshape(flat_shape).astype(jnp.bfloat16)
    grad_key_all = jnp.stack(key_grads, axis=1).reshape(flat_shape).astype(jnp.bfloat16)
    grad_value_all = jnp.stack(value_grads, axis=1).reshape(flat_shape).astype(jnp.bfloat16)
    grad_projected = jnp.stack([grad_query_all, grad_key_all, grad_value_all], axis=2)
    grad_w_qkv_part = jnp.einsum(
        "rsd,rsck->dck", gathered_one, grad_projected, preferred_element_type=jnp.float32
    )
    grad_b_qv = jnp.stack(
        [
            jnp.sum(grad_query_all, axis=(0, 1), dtype=jnp.float32),
            jnp.sum(grad_value_all, axis=(0, 1), dtype=jnp.float32),
        ]
    )
    picked = grad_projected
    grad_normed_one = lax.psum_scatter(
        jnp.einsum("rsck,dck->rsd", picked, w_qkv, preferred_element_type=jnp.float32).astype(
            jnp.bfloat16
        ),
        "heads",
        scatter_dimension=0,
        tiled=True,
    ).astype(jnp.float32)
    norm_one_back = jax.vjp(layer_norm, token_values, ln1_gain, ln1_bias)[1]
    grad_input, grad_gain_one, grad_shift_one = norm_one_back(grad_normed_one)
    grad_tokens = grad_input + grad_after + grad_direct.astype(jnp.float32)
    (
        grad_w_qkv_part,
        grad_b_qv,
        grad_w_out_part,
        grad_b_out,
        grad_gain_one,
        grad_shift_one,
        grad_w_up_part,
        grad_b_up,
        grad_w_down_part,
        grad_b_down,
        grad_gain_two,
        grad_shift_two,
    ) = (
        lax.psum(grad_w_qkv_part.astype(jnp.bfloat16), ("section", "rows")).astype(jnp.float32),
        lax.psum(grad_b_qv.astype(jnp.bfloat16), ("section", "rows")).astype(jnp.float32),
        lax.psum(grad_w_out_part.astype(jnp.bfloat16), ("section", "rows")).astype(jnp.float32),
        lax.psum(grad_b_out.astype(jnp.bfloat16), ("section", "rows")).astype(jnp.float32),
        lax.psum(grad_gain_one, ("section", "rows")).astype(jnp.float32),
        lax.psum(grad_shift_one, ("section", "rows")).astype(jnp.float32),
        lax.psum(grad_w_up_part.astype(jnp.bfloat16), ("section", "rows")).astype(jnp.float32),
        lax.psum(grad_b_up.astype(jnp.bfloat16), ("section", "rows")).astype(jnp.float32),
        lax.psum(grad_w_down_part.astype(jnp.bfloat16), ("section", "rows")).astype(jnp.float32),
        lax.psum(grad_b_down.astype(jnp.bfloat16), ("section", "rows")).astype(jnp.float32),
        lax.psum(grad_gain_two, ("section", "rows")).astype(jnp.float32),
        lax.psum(grad_shift_two, ("section", "rows")).astype(jnp.float32),
    )
    grad_b_out, grad_b_down, grad_gain_one, grad_shift_one, grad_gain_two, grad_shift_two = (
        lax.psum(
            (grad_b_out, grad_b_down, grad_gain_one, grad_shift_one, grad_gain_two, grad_shift_two),
            "heads",
        )
    )
    return (
        output_dec,
        tap_dec,
        grad_tokens[None],
        grad_w_qkv_part,
        grad_b_qv,
        grad_w_out_part,
        grad_b_out,
        grad_w_up_part,
        grad_b_up,
        grad_w_down_part,
        grad_b_down,
        grad_gain_one,
        grad_shift_one,
        grad_gain_two,
        grad_shift_two,
    )


def solution(mesh):
    placed = (
        P("section", "heads", "rows", None),
        P(None, "rows", None),
        P(None, "rows", None),
        P(None, None, "heads"),
        P(None, "heads"),
        P("heads", None),
        P(),
        P(None, "heads"),
        P("heads"),
        P("heads", None),
        P(),
        P(),
        P(),
        P(),
        P(),
        P(None, None, "rows", ("section", "heads")),
        P(None, None, "rows", ("section", "heads")),
    )
    return jax.shard_map(
        per_device,
        mesh=mesh,
        in_specs=placed,
        out_specs=(
            P(None, None, "rows", ("section", "heads")),
            P(None, None, "rows", ("section", "heads")),
            P("section", "heads", "rows", None),
            P(None, None, "heads"),
            P(None, "heads"),
            P("heads", None),
            P(),
            P(None, "heads"),
            P("heads"),
            P("heads", None),
            P(),
            P(),
            P(),
            P(),
            P(),
        ),
        check_vma=False,
    )
```

profile of v0, /device:TPU:0, one launch (start us, length us, event | category | flops | bytes accessed | tf_op | source)
XLA Modules:
  0.0 1077.3 jit_solution(13621030071722300098)
XLA Ops:
  17.5 35.0 %all-gather.5.cloned.1.call-done = bf16[2048,1,1024]{2,0,1:T(8,128)(2,1)} async-done(((bf16[512,1,1024]{2,0,1:T(8,128)(2,1)}), bf16[2048,1,1024]{2,0,1:T(8,128)(2,1)}) %all-gather.5.cloned.1.call-update) | async-done | bytes 4194320 | tf_op jit(solution)/shard_map/all_gather | solution.py:161
  52.5 5.8 fusion.115
  69.9 62.9 %while.27 = (s32[]{:T(128)}, bf16[4,512,4,64]{1,3,2,0:T(8,128)(2,1)}, f32[4,4,512]{2,1,0:T(4,128)}, s32[4,512]{1,0:T(4,128)S(1)}, s32[1,2048]{1,0:T(1,128)S(1)},...) while((s32[]{:T(128)}, ...), condition=%wide.region_7.8_spmd, body=%wide.region_4.7_spmd.sunk | while | flops 1125120000 | bytes 70072528 | solution.py:78
  70.6 4.5 fusion.230
  75.1 4.4 fusion.231
  79.6 5.1 fusion.232
  86.3 4.5 fusion.230
  90.8 4.4 fusion.231
  95.3 5.1 fusion.232
  102.0 4.5 fusion.230
  106.5 4.4 fusion.231
  111.0 5.1 fusion.232
  117.7 4.5 fusion.230
  122.2 4.4 fusion.231
  126.6 5.1 fusion.232
  139.7 44.5 %reduce-scatter.5.cloned.1.call-done = bf16[512,1,1024]{2,0,1:T(8,128)(2,1)} async-done(((bf16[2048,1,1024]{2,0,1:T(8,128)(2,1)}), bf16[512,1,1024]{2,0,1:T(8,128)(2,1)}) %reduce-scatter.5.cloned.1.call-update) | async-done | bytes 1048592 | tf_op jit(solution)/shard_map/reduce_scatter | solution.py:188
  191.5 7.9 fusion.130
  212.9 22.5 %all-to-all-done.2 = bf16[8,2,32768]{2,1,0:T(2,128)(2,1)} async-done(((bf16[8,2,32768]{2,1,0:T(2,128)(2,1)}), bf16[8,2,32768]{2,1,0:T(2,128)(2,1)}, u32[]{:S(2)}, u32[]{:S(2)}) %all-to-all-start.2) | async-done | bytes 1048608 | tf_op jit(solution)/shard_map/all_to_all | solution.py:229
  235.3 5.8 reshape.983
  245.8 25.9 %multiply_convert_fusion.1 = (bf16[2048,1024]{1,0:T(8,128)(2,1)}, f32[2048,1024]{1,0:T(8,128)}, f32[2048,1024]{1,0:T(8,128)}) fusion(f32[1024]{0:T(1024)S(1)} %convert_element_type.441, bf16[1024,1024]{1,0:T(8,128)(2,1)S(1)} %copy-done, bf16[2048,1,1024]{2,0,1:T(8,128)(2,1)} %all-gather.7.cloned.1.call-done), kind=kOutput, calls=%fused_computation.81 | convolution fusion | flops 4433379328 | bytes 27267072 | tf_op jit(solution)/shard_map/rsd,df->rsf/dot_general | solution.py:202
  271.7 7.7 all-gather.9.cloned.1.call-done
  279.4 13.9 %fusion.186 = (bf16[1024]{0:T(1024)(128)(2,1)}, bf16[2048,1024]{1,0:T(8,128)(2,1)S(1)}) fusion(f32[2048,1024]{1,0:T(8,128)} %get-tuple-element.358, bf16[1024,1024]{1,0:T(8,128)(2,1)} %param.30, bf16[2048,1,1024]{2,0,1:T(8,128)(2,1)} %all-gather.9.cloned.1.call-done, f32[2048,1024]{1,0:T(8,128)} %get-tuple-element.369, f32[1024]{0:T(1024)S(1)} %convert_element_type.441), kind=kOutput, calls=%fused_computation.215 | convolution fusion | flops 4328520704 | bytes 27269120 | tf_op jit(solution)/shard_map/rsd,fd->rsf/dot_general | solution.py:251
  295.3 6.1 convert_bitcast_fusion
  303.0 8.8 convert_bitcast_fusion.1
  312.4 33.6 %reduce-scatter.9.cloned.1.call-done = bf16[512,1,1024]{2,0,1:T(8,128)(2,1)} async-done(((bf16[2048,1,1024]{2,0,1:T(8,128)(2,1)}), bf16[512,1,1024]{2,0,1:T(8,128)(2,1)}) %reduce-scatter.9.cloned.1.call-update) | async-done | bytes 1048592 | tf_op jit(solution)/shard_map/reduce_scatter | solution.py:259
  348.0 45.0 %reduce-scatter.7.cloned.1.call-done = bf16[512,1,1024]{2,0,1:T(8,128)(2,1)} async-done(((bf16[2048,1,1024]{2,0,1:T(8,128)(2,1)}), bf16[512,1,1024]{2,0,1:T(8,128)(2,1)}) %reduce-scatter.7.cloned.1.call-update) | async-done | bytes 1048592 | tf_op jit(solution)/shard_map/reduce_scatter | solution.py:207
  393.0 4.6 fusion.141
  400.9 9.5 fusion.150
  410.4 5.8 fusion.147
  416.2 19.3 %all-gather.11.cloned.1.call-done = bf16[2048,1,1024]{2,0,1:T(8,128)(2,1)} async-done(((bf16[512,1,1024]{2,0,1:T(8,128)(2,1)}), bf16[2048,1,1024]{2,0,1:T(8,128)(2,1)}) %all-gather.11.cloned.1.call-update) | async-done | bytes 4194320 | tf_op jit(solution)/shard_map/all_gather | solution.py:272
  445.9 282.8 %while.28 = (s32[]{:T(128)}, f32[2048,4,64]{0,2,1:T(8,128)}, f32[2048,4,64]{0,2,1:T(8,128)}, bf16[4,512,4,64]{1,3,2,0:T(8,128)(2,1)}, bf16[4,512,4,64]{1,3,2,0:T...) while((s32[]{:T(128)}, f32[2048,4,64]{0,2,1:T(8,128)}, ...), condition=%wide.region_20.21_spmd.clone, body=%wide.region_18.20_spmd.clone.sunk | while | flops 2796560384 | bytes 275323104 | solution.py:112
  450.9 6.8 fusion.246
  457.7 8.1 fusion.243
  465.8 24.0 %fusion.247 = bf16[4,512,4,64]{1,3,2,0:T(8,128)(2,1)} fusion(bf16[4,512,4,64]{1,3,2,0:T(8,128)(2,1)} %get-tuple-element.537, s32[]{:T(128)S(6)} %copy.184, bf16[2048,4,64]{0,2,1:T(8,128)(2,1)S(1)} %get-tuple-element.554, f32[4,512,2048]{2,1,0:T(8,128)} %fusion.243, f32[4,512,2048]{2,1,0:T(8,128)} %copy-done.2, ...), kind=kOutput, calls=%fused_computation.42.clone.1 | convolution fusion | flops 583012352 | bytes 70795264 | tf_op jit(solution)/shard_map/while/body/eval_jaxpr/hqk,khd->qhd/dot_general | solution.py:100
  489.8 25.5 %fusion.245 = f32[2048,4,64]{0,2,1:T(8,128)} fusion(f32[4,512,2048]{2,1,0:T(8,128)} %fusion.243, f32[4,512,2048]{2,1,0:T(8,128)} %copy-done.2, f32[4,512]{1,0:T(4,128)S(1)} %dynamic-slice_bitcast_fusion.2, pred[512,2048]{1,0:T(8,128)(4,1)S(1)} %broadcast_compare_fusion.5, f32[2048,4,64]{0,2,1:T(8,128)} %get-tuple-element.535, pred[]{:T(512)S(6)} %compare.3, ...), kind=kOutput, calls=%fused_computation.39.clone.1 | convolution fusion | flops 584060928 | bytes 73678856 | tf_op jit(solution)/shard_map/while/body/eval_jaxpr/hqk,qhd->khd/dot_general | solution.py:103
  520.1 8.0 fusion.246
  528.1 8.1 fusion.243
  536.2 24.0 %fusion.247 = bf16[4,512,4,64]{1,3,2,0:T(8,128)(2,1)} fusion(bf16[4,512,4,64]{1,3,2,0:T(8,128)(2,1)} %get-tuple-element.537, s32[]{:T(128)S(6)} %copy.184, bf16[2048,4,64]{0,2,1:T(8,128)(2,1)S(1)} %get-tuple-element.554, f32[4,512,2048]{2,1,0:T(8,128)} %fusion.243, f32[4,512,2048]{2,1,0:T(8,128)} %copy-done.2, ...), kind=kOutput, calls=%fused_computation.42.clone.1 | convolution fusion | flops 583012352 | bytes 70795264 | tf_op jit(solution)/shard_map/while/body/eval_jaxpr/hqk,khd->qhd/dot_general | solution.py:100
  560.2 26.1 %fusion.245 = f32[2048,4,64]{0,2,1:T(8,128)} fusion(f32[4,512,2048]{2,1,0:T(8,128)} %fusion.243, f32[4,512,2048]{2,1,0:T(8,128)} %copy-done.2, f32[4,512]{1,0:T(4,128)S(1)} %dynamic-slice_bitcast_fusion.2, pred[512,2048]{1,0:T(8,128)(4,1)S(1)} %broadcast_compare_fusion.5, f32[2048,4,64]{0,2,1:T(8,128)} %get-tuple-element.535, pred[]{:T(512)S(6)} %compare.3, ...), kind=kOutput, calls=%fused_computation.39.clone.1 | convolution fusion | flops 584060928 | bytes 73678856 | tf_op jit(solution)/shard_map/while/body/eval_jaxpr/hqk,qhd->khd/dot_general | solution.py:103
  591.1 8.0 fusion.246
  599.1 8.1 fusion.243
  607.2 24.0 %fusion.247 = bf16[4,512,4,64]{1,3,2,0:T(8,128)(2,1)} fusion(bf16[4,512,4,64]{1,3,2,0:T(8,128)(2,1)} %get-tuple-element.537, s32[]{:T(128)S(6)} %copy.184, bf16[2048,4,64]{0,2,1:T(8,128)(2,1)S(1)} %get-tuple-element.554, f32[4,512,2048]{2,1,0:T(8,128)} %fusion.243, f32[4,512,2048]{2,1,0:T(8,128)} %copy-done.2, ...), kind=kOutput, calls=%fused_computation.42.clone.1 | convolution fusion | flops 583012352 | bytes 70795264 | tf_op jit(solution)/shard_map/while/body/eval_jaxpr/hqk,khd->qhd/dot_general | solution.py:100
  631.2 26.1 %fusion.245 = f32[2048,4,64]{0,2,1:T(8,128)} fusion(f32[4,512,2048]{2,1,0:T(8,128)} %fusion.243, f32[4,512,2048]{2,1,0:T(8,128)} %copy-done.2, f32[4,512]{1,0:T(4,128)S(1)} %dynamic-slice_bitcast_fusion.2, pred[512,2048]{1,0:T(8,128)(4,1)S(1)} %broadcast_compare_fusion.5, f32[2048,4,64]{0,2,1:T(8,128)} %get-tuple-element.535, pred[]{:T(512)S(6)} %compare.3, ...), kind=kOutput, calls=%fused_computation.39.clone.1 | convolution fusion | flops 584060928 | bytes 73678856 | tf_op jit(solution)/shard_map/while/body/eval_jaxpr/hqk,qhd->khd/dot_general | solution.py:103
  662.1 8.0 fusion.246
  670.1 8.1 fusion.243
  678.2 24.0 %fusion.247 = bf16[4,512,4,64]{1,3,2,0:T(8,128)(2,1)} fusion(bf16[4,512,4,64]{1,3,2,0:T(8,128)(2,1)} %get-tuple-element.537, s32[]{:T(128)S(6)} %copy.184, bf16[2048,4,64]{0,2,1:T(8,128)(2,1)S(1)} %get-tuple-element.554, f32[4,512,2048]{2,1,0:T(8,128)} %fusion.243, f32[4,512,2048]{2,1,0:T(8,128)} %copy-done.2, ...), kind=kOutput, calls=%fused_computation.42.clone.1 | convolution fusion | flops 583012352 | bytes 70795264 | tf_op jit(solution)/shard_map/while/body/eval_jaxpr/hqk,khd->qhd/dot_general | solution.py:100
  702.2 26.1 %fusion.245 = f32[2048,4,64]{0,2,1:T(8,128)} fusion(f32[4,512,2048]{2,1,0:T(8,128)} %fusion.243, f32[4,512,2048]{2,1,0:T(8,128)} %copy-done.2, f32[4,512]{1,0:T(4,128)S(1)} %dynamic-slice_bitcast_fusion.2, pred[512,2048]{1,0:T(8,128)(4,1)S(1)} %broadcast_compare_fusion.5, f32[2048,4,64]{0,2,1:T(8,128)} %get-tuple-element.535, pred[]{:T(512)S(6)} %compare.3, ...), kind=kOutput, calls=%fused_computation.39.clone.1 | convolution fusion | flops 584060928 | bytes 73678856 | tf_op jit(solution)/shard_map/while/body/eval_jaxpr/hqk,qhd->khd/dot_general | solution.py:103
  738.6 4.4 fusion.160
  743.0 4.7 fusion.154
  749.0 7.1 fusion.118
  757.3 6.8 fusion.131
  768.0 4.4 all-to-all-start.3
  776.3 9.2 reduce.38
  788.1 4.2 all-to-all-start.1
  796.2 8.0 reduce.37
  805.8 4.6 all-to-all-done.1
  814.3 5.8 reshape.989
  822.8 5.8 reshape.987
  833.6 7.9 fusion.135
  848.3 8.6 fusion.136
  858.6 103.7 %all-reduce.5.cloned.1.call-done = (bf16[1024,3,256]{2,0,1:T(8,128)(2,1)}, bf16[256,1024]{1,0:T(8,128)(2,1)}, bf16[1024,1024]{1,0:T(8,128)(2,1)}, bf16[1024,1024]{1,0:T(8,128)(2,1)}) async-done(((bf16[1024,3,256]{2,0,1:T(8,128)(2,1)}, bf16[256,1024]{1,0:T(8,128)(2,1)}, bf16[1024,1024]{1,0:T(8,128)(2,1)}, bf16[1024,1024]{1,0:T(8,128)(2,1)}), (bf16[1024,3,256]{2,0,1:T(8,128)(2,1)}, ...) | async-done | bytes 6291472 | tf_op jit(solution)/shard_map/psum | solution.py:334
  973.4 35.0 %reduce-scatter.11.cloned.1.call-done = bf16[512,1,1024]{2,0,1:T(8,128)(2,1)} async-done(((bf16[2048,1,1024]{2,0,1:T(8,128)(2,1)}), bf16[512,1,1024]{2,0,1:T(8,128)(2,1)}) %reduce-scatter.11.cloned.1.call-update) | async-done | bytes 1048592 | tf_op jit(solution)/shard_map/reduce_scatter | solution.py:309
  1014.0 37.5 %all-reduce.1 = (bf16[1024]{0:T(1024)(128)(2,1)S(1)}, bf16[1024]{0:T(1024)(128)(2,1)S(1)}, bf16[1024]{0:T(1024)(128)(2,1)S(1)}, bf16[1024]{0:T(1024)(128)(2,1)S(...) all-reduce(bf16[1024]{0:T(1024)(128)(2,1)S(1)} %copy-done.48, ...), channel_id=1, replica_groups=mesh['section'=2,'rows'=4,'heads'=4] {'section','rows'}, use_global_device_ids=true, to_apply=%region_30.31 | all-reduce | flops 7680 | bytes 30720 | tf_op jit(solution)/shard_map/psum | solution.py:337
  1059.4 10.9 %all-reduce = (f32[1024]{0:T(1024)}, f32[1024]{0:T(1024)}, f32[1024]{0:T(1024)}, f32[1024]{0:T(1024)}, f32[1024]{0:T(1024)}, /*index=5*/f32[1024]{0:T(1024)}) all-reduce(bf16[1024]{0:T(1024)(128)(2,1)S(1)} %get-tuple-element.338, ...), channel_id=1, replica_groups=mesh['section'=2,'rows'=4,'heads'=4] {'heads'}, use_global_device_ids=true, to_apply=%region_31.32 | all-reduce | flops 6144 | bytes 36864 | tf_op jit(solution)/shard_map/psum | solution.py:348
  (313 shorter events, 172.1 us)
Async XLA Ops:
  7.2 238.6 %copy-start = (bf16[1024,1024]{1,0:T(8,128)(2,1)S(1)}, bf16[1024,1024]{1,0:T(8,128)(2,1)}, u32[]{:S(2)}) copy-start(bf16[1024,1024]{1,0:T(8,128)(2,1)} %param.28) | copy-start | bytes 6291460
  7.2 8.0 copy-start.51
  7.2 8.2 copy-start.44
  7.2 45.3 %all-gather.5.cloned.1.call-start = ((), (), s32[]{:S(2)}) async-start(), calls=%async_computation.8 | async-start | bytes 5242880 | tf_op jit(solution)/shard_map/all_gather | solution.py:161
  8.8 7.4 copy-start.31
  11.8 4.5 copy-start.27
  15.1 169.1 %reduce-scatter.5.cloned.1.call-start = ((), (), s32[]{:S(2)}) async-start(), calls=%async_computation.9 | async-start | bytes 5242880 | tf_op jit(solution)/shard_map/reduce_scatter | solution.py:188
  16.1 36.4 %copy-start.34 = (s32[2,6]{0,1:T(8,128)}, s32[2,6]{0,1:T(8,128)S(1)}, u32[]{:S(2)}) copy-start(s32[2,6]{0,1:T(8,128)S(1)} %reduce_window_sum.11) | copy-start | bytes 148
  16.3 36.2 %copy-start.29 = (s32[2,2048]{1,0:T(2,128)}, s32[2,2048]{1,0:T(2,128)S(1)}, u32[]{:S(2)}) copy-start(s32[2,2048]{1,0:T(2,128)S(1)} %fusion.165) | copy-start | bytes 49156
  75.1 4.4 copy-start.8
  75.1 4.4 copy-start.17
  90.8 4.4 copy-start.8
  90.8 4.4 copy-start.17
  106.5 4.4 copy-start.8
  106.5 4.4 copy-start.17
  122.2 4.4 copy-start.8
  139.5 106.2 %all-gather.7.cloned.1.call-start = ((), (), s32[]{:S(2)}) async-start(), calls=%async_computation.10 | async-start | bytes 5242880 | tf_op jit(solution)/shard_map/all_gather | solution.py:200
  139.7 50.4 %copy-start.50 = (s32[2,1,6]{2,1,0:T(1,128)S(1)}, s32[2,1,6]{2,1,0:T(1,128)}, u32[]{:S(2)}) copy-start(s32[2,1,6]{2,1,0:T(1,128)} %param.23) | copy-start | bytes 148
  139.7 50.5 %copy-start.45 = (s32[2,1,6]{2,1,0:T(1,128)S(1)}, s32[2,1,6]{2,1,0:T(1,128)}, u32[]{:S(2)}) copy-start(s32[2,1,6]{2,1,0:T(1,128)} %param.22) | copy-start | bytes 148
  139.7 50.9 %copy-start.35 = (s32[2,6]{0,1:T(8,128)S(1)}, s32[2,6]{0,1:T(8,128)}, u32[]{:S(2)}) copy-start(s32[2,6]{0,1:T(8,128)} %copy-done.34) | copy-start | bytes 148
  139.7 50.9 %copy-start.37 = (s32[2,6]{0,1:T(8,128)S(1)}, s32[2,6]{0,1:T(8,128)}, u32[]{:S(2)}) copy-start(s32[2,6]{0,1:T(8,128)} %copy-done.36) | copy-start | bytes 148
  139.7 50.9 %copy-start.30 = (s32[2,2048]{1,0:T(2,128)S(1)}, s32[2,2048]{1,0:T(2,128)}, u32[]{:S(2)}) copy-start(s32[2,2048]{1,0:T(2,128)} %copy-done.29) | copy-start | bytes 49156
  191.5 7.9 copy-start.42
  205.4 30.0 %all-to-all-start.2 = ((bf16[8,2,32768]{2,1,0:T(2,128)(2,1)}), bf16[8,2,32768]{2,1,0:T(2,128)(2,1)}, u32[]{:S(2)}, u32[]{:S(2)}) async-start(bf16[8,2,32768]{2,1,0:T(2,128)(2,1)} %reshape.982), calls=%async_computation.4 | async-start | bytes 2097152 | tf_op jit(solution)/shard_map/all_to_all | solution.py:229
  209.6 69.8 %all-gather.9.cloned.1.call-start = ((), (), s32[]{:S(2)}) async-start(), calls=%async_computation.12 | async-start | bytes 5242880 | tf_op jit(solution)/shard_map/all_gather | solution.py:247
  212.9 32.9 %copy-start.55 = (bf16[1024]{0:T(1024)(128)(2,1)S(1)}, bf16[1024]{0:T(1024)(128)(2,1)}, u32[]{:S(2)}) copy-start(bf16[1024]{0:T(1024)(128)(2,1)} %param.29) | copy-start | bytes 6148
  245.7 100.4 %reduce-scatter.9.cloned.1.call-start = ((), (), s32[]{:S(2)}) async-start(), calls=%async_computation.13 | async-start | bytes 5242880 | tf_op jit(solution)/shard_map/reduce_scatter | solution.py:259
  301.4 91.6 %reduce-scatter.7.cloned.1.call-start = ((), (), s32[]{:S(2)}) async-start(), calls=%async_computation.11 | async-start | bytes 5242880 | tf_op jit(solution)/shard_map/reduce_scatter | solution.py:207
  311.7 34.3 %copy-start.4 = (bf16[1,512,1,1024]{3,1,2,0:T(8,128)(2,1)S(1)}, bf16[1,512,1,1024]{3,1,2,0:T(8,128)(2,1)}, u32[]{:S(2)}) copy-start(bf16[1,512,1,1024]{3,1,2,0:T(8,128)(2,1)} %param.21) | copy-start | bytes 3145732
  311.7 34.3 %copy-start.7 = (bf16[512,1,1024]{2,0,1:T(8,128)(2,1)S(1)}, bf16[512,1,1024]{2,0,1:T(8,128)(2,1)}, u32[]{:S(2)}) copy-start(bf16[512,1,1024]{2,0,1:T(8,128)(2,1)} %reduce-scatter.5.cloned.1.call-done) | copy-start | bytes 3145732
  311.8 123.7 %all-gather.11.cloned.1.call-start = ((), (), s32[]{:S(2)}) async-start(), calls=%async_computation.14 | async-start | bytes 5242880 | tf_op jit(solution)/shard_map/all_gather | solution.py:272
  393.0 4.6 copy-start.12
  393.0 4.6 copy-start.13
  400.8 561.5 %all-reduce.5.cloned.1.call-start = ((), (), s32[]{:S(2)}) async-start(), calls=%async_computation.16 | async-start | bytes 12582912 | tf_op jit(solution)/shard_map/psum | solution.py:334
  400.9 9.5 copy-start.59
  400.9 9.5 copy-start.65
  410.4 25.1 %copy-start.63 = (bf16[256,1024]{1,0:T(8,128)(2,1)S(1)}, bf16[256,1024]{1,0:T(8,128)(2,1)}, u32[]{:S(2)}) copy-start(bf16[256,1024]{1,0:T(8,128)(2,1)} %param.26) | copy-start | bytes 1572868
  439.0 7.0 copy-start.9
  450.9 6.8 copy-start.2
  520.1 8.1 copy-start.2
  591.1 8.1 copy-start.2
  662.1 8.1 copy-start.2
  738.6 4.4 copy-start.21
  738.6 4.4 copy-start.24
  738.6 4.4 copy-start.26
  738.6 4.4 copy-start.58
  747.8 260.6 %reduce-scatter.11.cloned.1.call-start = ((), (), s32[]{:S(2)}) async-start(), calls=%async_computation.15 | async-start | bytes 5242880 | tf_op jit(solution)/shard_map/reduce_scatter | solution.py:309
  764.1 8.3 copy-start.5
  768.0 20.1 %all-to-all-start.3 = ((bf16[8,2,32768]{2,1,0:T(2,128)(2,1)}), bf16[8,2,32768]{2,1,0:T(2,128)(2,1)}, u32[]{:S(2)}, u32[]{:S(2)}) async-start(bf16[8,2,32768]{2,1,0:T(2,128)(2,1)} %reshape.988), calls=%async_computation.7 | async-start | bytes 2097152 | tf_op jit(solution)/shard_map/all_to_all | solution.py:236
  776.3 16.0 %copy-start.16 = (bf16[512,1,1024]{2,0,1:T(8,128)(2,1)S(1)}, bf16[512,1,1024]{2,0,1:T(8,128)(2,1)}, u32[]{:S(2)}) copy-start(bf16[512,1,1024]{2,0,1:T(8,128)(2,1)} %get-tuple-element.365) | copy-start | bytes 3145732
  788.1 22.4 %all-to-all-start.1 = ((bf16[8,2,32768]{2,1,0:T(2,128)(2,1)}), bf16[8,2,32768]{2,1,0:T(2,128)(2,1)}, u32[]{:S(2)}, u32[]{:S(2)}) async-start(bf16[8,2,32768]{2,1,0:T(2,128)(2,1)} %reshape.986), calls=%async_computation.3 | async-start | bytes 2097152 | tf_op jit(solution)/shard_map/all_to_all | solution.py:220
  796.2 18.0 %copy-start.33 = (s32[2,2048]{1,0:T(2,128)S(1)}, s32[2,2048]{1,0:T(2,128)}, u32[]{:S(2)}) copy-start(s32[2,2048]{1,0:T(2,128)} %get-tuple-element.373) | copy-start | bytes 49156
  810.5 31.1 %all-to-all-start = ((bf16[8,2,32768]{2,1,0:T(2,128)(2,1)}), bf16[8,2,32768]{2,1,0:T(2,128)(2,1)S(1)}, u32[]{:S(2)}, u32[]{:S(2)}) async-start(bf16[8,2,32768]{2,1,0:T(2,128)(2,1)} %reshape.984), calls=%async_computation.2 | async-start | bytes 2097152 | tf_op jit(solution)/shard_map/all_to_all | solution.py:219
  962.3 5.6 copy-start.20
  970.4 37.9 %copy-start.28 = (f32[1024]{0:T(1024)S(1)}, f32[1024]{0:T(1024)}, u32[]{:S(2)}) copy-start(f32[1024]{0:T(1024)} %copy-done.27) | copy-start | bytes 12292
  970.4 37.9 %copy-start.32 = (f32[512]{0:T(512)S(1)}, f32[512]{0:T(512)}, u32[]{:S(2)}) copy-start(f32[512]{0:T(512)} %copy-done.31) | copy-start | bytes 6148
  970.4 39.7 %copy-start.41 = (f32[512]{0:T(512)S(1)}, f32[512]{0:T(512)}, u32[]{:S(2)}) copy-start(f32[512]{0:T(512)} %copy-done.40) | copy-start | bytes 6148
  970.5 41.1 %copy-start.39 = (f32[512]{0:T(512)S(1)}, f32[512]{0:T(512)}, u32[]{:S(2)}) copy-start(f32[512]{0:T(512)} %copy-done.38) | copy-start | bytes 6148
  973.4 40.6 %copy-start.46 = (bf16[1024]{0:T(1024)(128)(2,1)S(1)}, bf16[1024]{0:T(1024)(128)(2,1)}, u32[]{:S(2)}) copy-start(bf16[1024]{0:T(1024)(128)(2,1)} %get-tuple-element.288) | copy-start | bytes 6148
  973.4 40.6 %copy-start.47 = (bf16[1024]{0:T(1024)(128)(2,1)S(1)}, bf16[1024]{0:T(1024)(128)(2,1)}, u32[]{:S(2)}) copy-start(bf16[1024]{0:T(1024)(128)(2,1)} %get-tuple-element.352) | copy-start | bytes 6148
  973.4 40.6 %copy-start.48 = (bf16[1024]{0:T(1024)(128)(2,1)S(1)}, bf16[1024]{0:T(1024)(128)(2,1)}, u32[]{:S(2)}) copy-start(bf16[1024]{0:T(1024)(128)(2,1)} %get-tuple-element.354) | copy-start | bytes 6148
  973.4 40.6 %copy-start.49 = (bf16[1024]{0:T(1024)(128)(2,1)S(1)}, bf16[1024]{0:T(1024)(128)(2,1)}, u32[]{:S(2)}) copy-start(bf16[1024]{0:T(1024)(128)(2,1)} %get-tuple-element.366) | copy-start | bytes 6148
  973.4 40.6 %copy-start.57 = (bf16[1024]{0:T(1024)(128)(2,1)S(1)}, bf16[1024]{0:T(1024)(128)(2,1)}, u32[]{:S(2)}) copy-start(bf16[1024]{0:T(1024)(128)(2,1)} %get-tuple-element.370) | copy-start | bytes 6148
  1052.1 18.2 %copy-start.1 = (bf16[1024,1024]{1,0:T(8,128)(2,1)S(1)}, bf16[1024,1024]{1,0:T(8,128)(2,1)}, u32[]{:S(2)}) copy-start(bf16[1024,1024]{1,0:T(8,128)(2,1)} %param.28) | copy-start | bytes 6291460
  (30 other events, 70.8 us)
Sparse Core Ops, SparseCore 0:
  15.3 37.1 all-gather.4
  139.7 44.4 reduce-scatter.4
  190.2 44.9 all-gather.6
  245.8 33.5 all-gather.8
  301.5 44.4 reduce-scatter.8
  348.4 44.4 reduce-scatter.6
  401.0 34.4 all-gather.10
  747.9 214.4 all-reduce.4
  964.9 43.4 reduce-scatter.10
where the time goes:
time: 1090 us; the launch traced here: 1080 us
  matrix products  445 us (41%)
  waiting for transfers between devices  351 us (32%)
  other arithmetic  104 us (10%)
  local copies, waits for them, and re-layouts  95.7 us (9%)
  blocking collectives  48.4 us (4%)
  starting transfers between devices  17.1 us (2%)
  between operations  15 us (1%)
    psum x1, waiting for transfers between devices, per_device(): lax.psum(grad_w_qkv_part.astype(jnp.bfloat16), ('section', 'rows'))  104 us
    dot_general x4, matrix products, one_block(): jnp.einsum('hqk,qhd->khd', grad_score, queries, preferred_element_type=jn...  104 us
    dot_general x4, matrix products, one_block(): jnp.einsum('hqk,khd->qhd', grad_score, key_seq, preferred_element_type=jn...  96 us
    unnamed x136, local copies, waits for them, and re-layouts  51.9 us
    reduce_scatter x1, waiting for transfers between devices, per_device(): lax.psum_scatter(jnp.einsum('rsf,fd->rsd', picked, w_down, preferred_elem...  45 us
    reduce_scatter x1, waiting for transfers between devices, per_device(): lax.psum_scatter(jnp.einsum('rsk,kd->rsd', picked, w_out, preferred_eleme...  44.5 us
    psum x1, blocking collectives, per_device(): lax.psum(grad_b_out.astype(jnp.bfloat16), ('section', 'rows'))  37.5 us
    all_gather x1, waiting for transfers between devices, per_device(): gathered_one = lax.all_gather(normed_one, 'heads', axis=0, tiled=True)  35 us
  transfers between devices with their start and end apart: 13, of which 10 were waited for; matrix products, arithmetic and copies ran while one was open for 17% of the time, Pallas kernels for 0%

commit v1 on v0

--- a/solution.py
+++ b/solution.py
@@ -226,12 +226,18 @@
     encoder_shape = (halves * full_len, seq_count, grad_out.shape[3])
     back_out, back_tap = reorder_pair(grad_out, grad_tap, targets)
     grad_block, grad_direct = (
-        lax.all_to_all(
-            back_out.reshape(encoder_shape),
-            ("section", "heads"),
-            split_axis=0,
-            concat_axis=2,
-            tiled=True,
+        jnp.concatenate(
+            lax.all_to_all(
+                jnp.stack(
+                    jnp.split(
+                        back_out.reshape(encoder_shape), lax.axis_size(("section", "heads")), axis=0
+                    )
+                ),
+                ("section", "heads"),
+                0,
+                0,
+            ),
+            axis=2,
         ),
         lax.all_to_all(
             back_tap.reshape(encoder_shape),

time: 1090 us -> 1080 us (level)
    unnamed x136 -> x138, local copies, waits for them, and re-layouts: 51.9 us -> 48.1 us
  transfers between devices with their start and end apart: 13 -> 13, of which waited for: 10 -> 10; matrix products, arithmetic and copies ran while one was open for 17% -> 16% of each run, Pallas kernels for 0% -> 0%
where the time goes in v1:
time: 1080 us; the launch traced here: 1070 us
  matrix products  444 us (41%)
  waiting for transfers between devices  353 us (33%)
  other arithmetic  103 us (10%)
  local copies, waits for them, and re-layouts  90.3 us (8%)
  blocking collectives  48.4 us (4%)
  starting transfers between devices  17.1 us (2%)
  between operations  15 us (1%)
    dot_general x4, matrix products, one_block(): jnp.einsum('hqk,qhd->khd', grad_score, queries, preferred_element_type=jn...  104 us
    psum x1, waiting for transfers between devices, per_device(): lax.psum(grad_w_qkv_part.astype(jnp.bfloat16), ('section', 'rows'))  104 us
    dot_general x4, matrix products, one_block(): jnp.einsum('hqk,khd->qhd', grad_score, key_seq, preferred_element_type=jn...  96 us
    unnamed x138, local copies, waits for them, and re-layouts  48.1 us
    reduce_scatter x1, waiting for transfers between devices, per_device(): lax.psum_scatter(jnp.einsum('rsf,fd->rsd', picked, w_down, preferred_elem...  45 us
    reduce_scatter x1, waiting for transfers between devices, per_device(): lax.psum_scatter(jnp.einsum('rsk,kd->rsd', picked, w_out, preferred_eleme...  44.5 us
    psum x1, blocking collectives, per_device(): lax.psum(grad_b_out.astype(jnp.bfloat16), ('section', 'rows'))  37.5 us
    all_gather x1, waiting for transfers between devices, per_device(): gathered_one = lax.all_gather(normed_one, 'heads', axis=0, tiled=True)  35 us
  transfers between devices with their start and end apart: 13, of which 10 were waited for; matrix products, arithmetic and copies ran while one was open for 16% of the time, Pallas kernels for 0%

profile of v1, /device:TPU:0, one launch (start us, length us, event | category | flops | bytes accessed | tf_op | source)
XLA Modules:
  0.0 1071.4 jit_solution(9753714632724897030)
XLA Ops:
  17.5 35.0 %all-gather.5.cloned.1.call-done = bf16[2048,1,1024]{2,0,1:T(8,128)(2,1)} async-done(((bf16[512,1,1024]{2,0,1:T(8,128)(2,1)}), bf16[2048,1,1024]{2,0,1:T(8,128)(2,1)}) %all-gather.5.cloned.1.call-update) | async-done | bytes 4194320 | tf_op jit(solution)/shard_map/all_gather | solution.py:161
  52.5 5.8 fusion.115
  69.9 62.9 %while.27 = (s32[]{:T(128)}, bf16[4,512,4,64]{1,3,2,0:T(8,128)(2,1)}, f32[4,4,512]{2,1,0:T(4,128)}, s32[4,512]{1,0:T(4,128)S(1)}, s32[1,2048]{1,0:T(1,128)S(1)},...) while((s32[]{:T(128)}, ...), condition=%wide.region_7.8_spmd, body=%wide.region_4.7_spmd.sunk | while | flops 1125120000 | bytes 70072528 | solution.py:78
  70.6 4.5 fusion.238
  75.1 4.4 fusion.239
  79.6 5.1 fusion.240
  86.3 4.5 fusion.238
  90.8 4.4 fusion.239
  95.2 5.1 fusion.240
  102.0 4.5 fusion.238
  106.5 4.4 fusion.239
  110.9 5.1 fusion.240
  117.6 4.5 fusion.238
  122.2 4.4 fusion.239
  126.6 5.1 fusion.240
  139.7 44.5 %reduce-scatter.5.cloned.1.call-done = bf16[512,1,1024]{2,0,1:T(8,128)(2,1)} async-done(((bf16[2048,1,1024]{2,0,1:T(8,128)(2,1)}), bf16[512,1,1024]{2,0,1:T(8,128)(2,1)}) %reduce-scatter.5.cloned.1.call-update) | async-done | bytes 1048592 | tf_op jit(solution)/shard_map/reduce_scatter | solution.py:188
  191.5 7.1 fusion.130
  203.9 4.3 all-to-all-start.2
  211.4 23.7 %all-to-all-done.2 = bf16[8,512,1,128]{3,1,2,0:T(8,128)(2,1)} async-done(((bf16[8,512,1,128]{3,1,2,0:T(8,128)(2,1)}), bf16[8,512,1,128]{3,1,2,0:T(8,128)(2,1)}, u32[]{:S(2)}, u32[]{:S(2)}) %all-to-all-start.2) | async-done | bytes 1048608 | tf_op jit(solution)/shard_map/all_to_all | solution.py:230
  238.3 25.9 %multiply_convert_fusion.1 = (bf16[2048,1024]{1,0:T(8,128)(2,1)}, f32[2048,1024]{1,0:T(8,128)}, f32[2048,1024]{1,0:T(8,128)}) fusion(f32[1024]{0:T(1024)S(1)} %convert_element_type.438, bf16[1024,1024]{1,0:T(8,128)(2,1)S(1)} %copy-done, bf16[2048,1,1024]{2,0,1:T(8,128)(2,1)} %all-gather.7.cloned.1.call-done), kind=kOutput, calls=%fused_computation.81 | convolution fusion | flops 4433379328 | bytes 27267072 | tf_op jit(solution)/shard_map/rsd,df->rsf/dot_general | solution.py:202
  264.2 8.3 all-gather.9.cloned.1.call-done
  272.5 13.9 %fusion.194 = (bf16[1024]{0:T(1024)(128)(2,1)}, bf16[2048,1024]{1,0:T(8,128)(2,1)S(1)}) fusion(f32[2048,1024]{1,0:T(8,128)} %get-tuple-element.358, bf16[1024,1024]{1,0:T(8,128)(2,1)} %param.30, bf16[2048,1,1024]{2,0,1:T(8,128)(2,1)} %all-gather.9.cloned.1.call-done, f32[2048,1024]{1,0:T(8,128)} %get-tuple-element.369, f32[1024]{0:T(1024)S(1)} %convert_element_type.438), kind=kOutput, calls=%fused_computation.231 | convolution fusion | flops 4328520704 | bytes 27269120 | tf_op jit(solution)/shard_map/rsd,fd->rsf/dot_general | solution.py:257
  288.3 6.1 convert_bitcast_fusion
  296.0 8.8 convert_bitcast_fusion.1
  305.5 33.6 %reduce-scatter.9.cloned.1.call-done = bf16[512,1,1024]{2,0,1:T(8,128)(2,1)} async-done(((bf16[2048,1,1024]{2,0,1:T(8,128)(2,1)}), bf16[512,1,1024]{2,0,1:T(8,128)(2,1)}) %reduce-scatter.9.cloned.1.call-update) | async-done | bytes 1048592 | tf_op jit(solution)/shard_map/reduce_scatter | solution.py:265
  341.1 45.0 %reduce-scatter.7.cloned.1.call-done = bf16[512,1,1024]{2,0,1:T(8,128)(2,1)} async-done(((bf16[2048,1,1024]{2,0,1:T(8,128)(2,1)}), bf16[512,1,1024]{2,0,1:T(8,128)(2,1)}) %reduce-scatter.7.cloned.1.call-update) | async-done | bytes 1048592 | tf_op jit(solution)/shard_map/reduce_scatter | solution.py:207
  386.0 4.6 fusion.141
  390.6 4.3 fusion.190
  395.0 9.5 fusion.150
  404.5 5.8 fusion.147
  410.2 19.3 %all-gather.11.cloned.1.call-done = bf16[2048,1,1024]{2,0,1:T(8,128)(2,1)} async-done(((bf16[512,1,1024]{2,0,1:T(8,128)(2,1)}), bf16[2048,1,1024]{2,0,1:T(8,128)(2,1)}) %all-gather.11.cloned.1.call-update) | async-done | bytes 4194320 | tf_op jit(solution)/shard_map/all_gather | solution.py:278
  440.0 282.8 %while.28 = (s32[]{:T(128)}, f32[2048,4,64]{0,2,1:T(8,128)}, f32[2048,4,64]{0,2,1:T(8,128)}, bf16[4,512,4,64]{1,3,2,0:T(8,128)(2,1)}, bf16[4,512,4,64]{1,3,2,0:T...) while((s32[]{:T(128)}, f32[2048,4,64]{0,2,1:T(8,128)}, ...), condition=%wide.region_20.21_spmd.clone, body=%wide.region_18.20_spmd.clone.sunk | while | flops 2796560384 | bytes 275323104 | solution.py:112
  444.9 6.8 fusion.254
  451.7 8.1 fusion.251
  459.8 24.0 %fusion.255 = bf16[4,512,4,64]{1,3,2,0:T(8,128)(2,1)} fusion(bf16[4,512,4,64]{1,3,2,0:T(8,128)(2,1)} %get-tuple-element.537, s32[]{:T(128)S(6)} %copy.191, bf16[2048,4,64]{0,2,1:T(8,128)(2,1)S(1)} %get-tuple-element.554, f32[4,512,2048]{2,1,0:T(8,128)} %fusion.251, f32[4,512,2048]{2,1,0:T(8,128)} %copy-done.2, ...), kind=kOutput, calls=%fused_computation.42.clone.1 | convolution fusion | flops 583012352 | bytes 70795264 | tf_op jit(solution)/shard_map/while/body/eval_jaxpr/hqk,khd->qhd/dot_general | solution.py:100
  483.8 25.5 %fusion.253 = f32[2048,4,64]{0,2,1:T(8,128)} fusion(f32[4,512,2048]{2,1,0:T(8,128)} %fusion.251, f32[4,512,2048]{2,1,0:T(8,128)} %copy-done.2, f32[4,512]{1,0:T(4,128)S(1)} %dynamic-slice_bitcast_fusion.2, pred[512,2048]{1,0:T(8,128)(4,1)S(1)} %broadcast_compare_fusion.5, f32[2048,4,64]{0,2,1:T(8,128)} %get-tuple-element.535, pred[]{:T(512)S(6)} %compare.3, ...), kind=kOutput, calls=%fused_computation.39.clone.1 | convolution fusion | flops 584060928 | bytes 73678856 | tf_op jit(solution)/shard_map/while/body/eval_jaxpr/hqk,qhd->khd/dot_general | solution.py:103
  514.1 8.0 fusion.254
  522.2 8.1 fusion.251
  530.3 24.0 %fusion.255 = bf16[4,512,4,64]{1,3,2,0:T(8,128)(2,1)} fusion(bf16[4,512,4,64]{1,3,2,0:T(8,128)(2,1)} %get-tuple-element.537, s32[]{:T(128)S(6)} %copy.191, bf16[2048,4,64]{0,2,1:T(8,128)(2,1)S(1)} %get-tuple-element.554, f32[4,512,2048]{2,1,0:T(8,128)} %fusion.251, f32[4,512,2048]{2,1,0:T(8,128)} %copy-done.2, ...), kind=kOutput, calls=%fused_computation.42.clone.1 | convolution fusion | flops 583012352 | bytes 70795264 | tf_op jit(solution)/shard_map/while/body/eval_jaxpr/hqk,khd->qhd/dot_general | solution.py:100
  554.2 26.1 %fusion.253 = f32[2048,4,64]{0,2,1:T(8,128)} fusion(f32[4,512,2048]{2,1,0:T(8,128)} %fusion.251, f32[4,512,2048]{2,1,0:T(8,128)} %copy-done.2, f32[4,512]{1,0:T(4,128)S(1)} %dynamic-slice_bitcast_fusion.2, pred[512,2048]{1,0:T(8,128)(4,1)S(1)} %broadcast_compare_fusion.5, f32[2048,4,64]{0,2,1:T(8,128)} %get-tuple-element.535, pred[]{:T(512)S(6)} %compare.3, ...), kind=kOutput, calls=%fused_computation.39.clone.1 | convolution fusion | flops 584060928 | bytes 73678856 | tf_op jit(solution)/shard_map/while/body/eval_jaxpr/hqk,qhd->khd/dot_general | solution.py:103
  585.1 8.0 fusion.254
  593.2 8.1 fusion.251
  601.3 24.0 %fusion.255 = bf16[4,512,4,64]{1,3,2,0:T(8,128)(2,1)} fusion(bf16[4,512,4,64]{1,3,2,0:T(8,128)(2,1)} %get-tuple-element.537, s32[]{:T(128)S(6)} %copy.191, bf16[2048,4,64]{0,2,1:T(8,128)(2,1)S(1)} %get-tuple-element.554, f32[4,512,2048]{2,1,0:T(8,128)} %fusion.251, f32[4,512,2048]{2,1,0:T(8,128)} %copy-done.2, ...), kind=kOutput, calls=%fused_computation.42.clone.1 | convolution fusion | flops 583012352 | bytes 70795264 | tf_op jit(solution)/shard_map/while/body/eval_jaxpr/hqk,khd->qhd/dot_general | solution.py:100
  625.3 26.1 %fusion.253 = f32[2048,4,64]{0,2,1:T(8,128)} fusion(f32[4,512,2048]{2,1,0:T(8,128)} %fusion.251, f32[4,512,2048]{2,1,0:T(8,128)} %copy-done.2, f32[4,512]{1,0:T(4,128)S(1)} %dynamic-slice_bitcast_fusion.2, pred[512,2048]{1,0:T(8,128)(4,1)S(1)} %broadcast_compare_fusion.5, f32[2048,4,64]{0,2,1:T(8,128)} %get-tuple-element.535, pred[]{:T(512)S(6)} %compare.3, ...), kind=kOutput, calls=%fused_computation.39.clone.1 | convolution fusion | flops 584060928 | bytes 73678856 | tf_op jit(solution)/shard_map/while/body/eval_jaxpr/hqk,qhd->khd/dot_general | solution.py:103
  656.2 8.0 fusion.254
  664.2 8.1 fusion.251
  672.3 24.0 %fusion.255 = bf16[4,512,4,64]{1,3,2,0:T(8,128)(2,1)} fusion(bf16[4,512,4,64]{1,3,2,0:T(8,128)(2,1)} %get-tuple-element.537, s32[]{:T(128)S(6)} %copy.191, bf16[2048,4,64]{0,2,1:T(8,128)(2,1)S(1)} %get-tuple-element.554, f32[4,512,2048]{2,1,0:T(8,128)} %fusion.251, f32[4,512,2048]{2,1,0:T(8,128)} %copy-done.2, ...), kind=kOutput, calls=%fused_computation.42.clone.1 | convolution fusion | flops 583012352 | bytes 70795264 | tf_op jit(solution)/shard_map/while/body/eval_jaxpr/hqk,khd->qhd/dot_general | solution.py:100
  696.3 26.1 %fusion.253 = f32[2048,4,64]{0,2,1:T(8,128)} fusion(f32[4,512,2048]{2,1,0:T(8,128)} %fusion.251, f32[4,512,2048]{2,1,0:T(8,128)} %copy-done.2, f32[4,512]{1,0:T(4,128)S(1)} %dynamic-slice_bitcast_fusion.2, pred[512,2048]{1,0:T(8,128)(4,1)S(1)} %broadcast_compare_fusion.5, f32[2048,4,64]{0,2,1:T(8,128)} %get-tuple-element.535, pred[]{:T(512)S(6)} %compare.3, ...), kind=kOutput, calls=%fused_computation.39.clone.1 | convolution fusion | flops 584060928 | bytes 73678856 | tf_op jit(solution)/shard_map/while/body/eval_jaxpr/hqk,qhd->khd/dot_general | solution.py:103
  732.7 4.4 fusion.160
  737.1 4.7 fusion.154
  743.0 7.1 fusion.118
  751.4 6.7 fusion.131
  762.3 4.4 all-to-all-start.3
  770.7 9.1 reduce.37
  790.5 8.0 reduce.36
  800.1 4.6 all-to-all-done.1
  808.5 5.8 reshape.986
  817.0 5.8 reshape.984
  827.9 7.9 fusion.135
  842.5 8.6 fusion.136
  852.8 103.6 %all-reduce.5.cloned.1.call-done = (bf16[1024,3,256]{2,0,1:T(8,128)(2,1)}, bf16[256,1024]{1,0:T(8,128)(2,1)}, bf16[1024,1024]{1,0:T(8,128)(2,1)}, bf16[1024,1024]{1,0:T(8,128)(2,1)}) async-done(((bf16[1024,3,256]{2,0,1:T(8,128)(2,1)}, bf16[256,1024]{1,0:T(8,128)(2,1)}, bf16[1024,1024]{1,0:T(8,128)(2,1)}, bf16[1024,1024]{1,0:T(8,128)(2,1)}), (bf16[1024,3,256]{2,0,1:T(8,128)(2,1)}, ...) | async-done | bytes 6291472 | tf_op jit(solution)/shard_map/psum | solution.py:340
  967.4 35.0 %reduce-scatter.11.cloned.1.call-done = bf16[512,1,1024]{2,0,1:T(8,128)(2,1)} async-done(((bf16[2048,1,1024]{2,0,1:T(8,128)(2,1)}), bf16[512,1,1024]{2,0,1:T(8,128)(2,1)}) %reduce-scatter.11.cloned.1.call-update) | async-done | bytes 1048592 | tf_op jit(solution)/shard_map/reduce_scatter | solution.py:315
  1008.1 37.5 %all-reduce.1 = (bf16[1024]{0:T(1024)(128)(2,1)S(1)}, bf16[1024]{0:T(1024)(128)(2,1)S(1)}, bf16[1024]{0:T(1024)(128)(2,1)S(1)}, bf16[1024]{0:T(1024)(128)(2,1)S(...) all-reduce(bf16[1024]{0:T(1024)(128)(2,1)S(1)} %copy-done.46, ...), channel_id=1, replica_groups=mesh['section'=2,'rows'=4,'heads'=4] {'section','rows'}, use_global_device_ids=true, to_apply=%region_30.31 | all-reduce | flops 7680 | bytes 30720 | tf_op jit(solution)/shard_map/psum | solution.py:343
  1053.5 10.9 %all-reduce = (f32[1024]{0:T(1024)}, f32[1024]{0:T(1024)}, f32[1024]{0:T(1024)}, f32[1024]{0:T(1024)}, f32[1024]{0:T(1024)}, /*index=5*/f32[1024]{0:T(1024)}) all-reduce(bf16[1024]{0:T(1024)(128)(2,1)S(1)} %get-tuple-element.338, ...), channel_id=1, replica_groups=mesh['section'=2,'rows'=4,'heads'=4] {'heads'}, use_global_device_ids=true, to_apply=%region_31.32 | all-reduce | flops 6144 | bytes 36864 | tf_op jit(solution)/shard_map/psum | solution.py:354
  (313 shorter events, 167.0 us)
Async XLA Ops:
  7.2 231.1 %copy-start = (bf16[1024,1024]{1,0:T(8,128)(2,1)S(1)}, bf16[1024,1024]{1,0:T(8,128)(2,1)}, u32[]{:S(2)}) copy-start(bf16[1024,1024]{1,0:T(8,128)(2,1)} %param.28) | copy-start | bytes 6291460
  7.2 8.0 copy-start.49
  7.2 8.2 copy-start.42
  7.2 45.2 %all-gather.5.cloned.1.call-start = ((), (), s32[]{:S(2)}) async-start(), calls=%async_computation.8 | async-start | bytes 5242880 | tf_op jit(solution)/shard_map/all_gather | solution.py:161
  8.8 7.4 copy-start.29
  11.8 4.5 copy-start.25
  15.1 169.0 %reduce-scatter.5.cloned.1.call-start = ((), (), s32[]{:S(2)}) async-start(), calls=%async_computation.9 | async-start | bytes 5242880 | tf_op jit(solution)/shard_map/reduce_scatter | solution.py:188
  16.1 36.4 %copy-start.32 = (s32[2,6]{0,1:T(8,128)}, s32[2,6]{0,1:T(8,128)S(1)}, u32[]{:S(2)}) copy-start(s32[2,6]{0,1:T(8,128)S(1)} %reduce_window_sum.11) | copy-start | bytes 148
  16.2 36.2 %copy-start.27 = (s32[2,2048]{1,0:T(2,128)}, s32[2,2048]{1,0:T(2,128)S(1)}, u32[]{:S(2)}) copy-start(s32[2,2048]{1,0:T(2,128)S(1)} %fusion.173) | copy-start | bytes 49156
  75.1 4.4 copy-start.8
  75.1 4.4 copy-start.15
  90.8 4.4 copy-start.8
  90.8 4.4 copy-start.15
  106.5 4.4 copy-start.8
  106.5 4.4 copy-start.15
  122.2 4.4 copy-start.8
  122.2 4.4 copy-start.15
  139.5 98.8 %all-gather.7.cloned.1.call-start = ((), (), s32[]{:S(2)}) async-start(), calls=%async_computation.10 | async-start | bytes 5242880 | tf_op jit(solution)/shard_map/all_gather | solution.py:200
  139.6 50.4 %copy-start.48 = (s32[2,1,6]{2,1,0:T(1,128)S(1)}, s32[2,1,6]{2,1,0:T(1,128)}, u32[]{:S(2)}) copy-start(s32[2,1,6]{2,1,0:T(1,128)} %param.23) | copy-start | bytes 148
  139.6 50.5 %copy-start.43 = (s32[2,1,6]{2,1,0:T(1,128)S(1)}, s32[2,1,6]{2,1,0:T(1,128)}, u32[]{:S(2)}) copy-start(s32[2,1,6]{2,1,0:T(1,128)} %param.22) | copy-start | bytes 148
  139.7 50.9 %copy-start.33 = (s32[2,6]{0,1:T(8,128)S(1)}, s32[2,6]{0,1:T(8,128)}, u32[]{:S(2)}) copy-start(s32[2,6]{0,1:T(8,128)} %copy-done.32) | copy-start | bytes 148
  139.7 50.9 %copy-start.35 = (s32[2,6]{0,1:T(8,128)S(1)}, s32[2,6]{0,1:T(8,128)}, u32[]{:S(2)}) copy-start(s32[2,6]{0,1:T(8,128)} %copy-done.34) | copy-start | bytes 148
  139.7 50.9 %copy-start.28 = (s32[2,2048]{1,0:T(2,128)S(1)}, s32[2,2048]{1,0:T(2,128)}, u32[]{:S(2)}) copy-start(s32[2,2048]{1,0:T(2,128)} %copy-done.27) | copy-start | bytes 49156
  191.4 7.1 copy-start.40
  201.2 37.0 %copy-start.53 = (bf16[1024]{0:T(1024)(128)(2,1)S(1)}, bf16[1024]{0:T(1024)(128)(2,1)}, u32[]{:S(2)}) copy-start(bf16[1024]{0:T(1024)(128)(2,1)} %param.29) | copy-start | bytes 6148
  203.9 31.2 %all-to-all-start.2 = ((bf16[8,512,1,128]{3,1,2,0:T(8,128)(2,1)}), bf16[8,512,1,128]{3,1,2,0:T(8,128)(2,1)}, u32[]{:S(2)}, u32[]{:S(2)}) async-start(bf16[8,512,1,128]{3,1,2,0:T(8,128)(2,1)} %fusion.165), calls=%async_computation.4 | async-start | bytes 2097152 | tf_op jit(solution)/shard_map/all_to_all | solution.py:230
  208.2 64.3 %all-gather.9.cloned.1.call-start = ((), (), s32[]{:S(2)}) async-start(), calls=%async_computation.12 | async-start | bytes 5242880 | tf_op jit(solution)/shard_map/all_gather | solution.py:253
  238.2 100.9 %reduce-scatter.9.cloned.1.call-start = ((), (), s32[]{:S(2)}) async-start(), calls=%async_computation.13 | async-start | bytes 5242880 | tf_op jit(solution)/shard_map/reduce_scatter | solution.py:265
  294.4 91.6 %reduce-scatter.7.cloned.1.call-start = ((), (), s32[]{:S(2)}) async-start(), calls=%async_computation.11 | async-start | bytes 5242880 | tf_op jit(solution)/shard_map/reduce_scatter | solution.py:207
  304.8 34.3 %copy-start.4 = (bf16[1,512,1,1024]{3,1,2,0:T(8,128)(2,1)S(1)}, bf16[1,512,1,1024]{3,1,2,0:T(8,128)(2,1)}, u32[]{:S(2)}) copy-start(bf16[1,512,1,1024]{3,1,2,0:T(8,128)(2,1)} %param.21) | copy-start | bytes 3145732
  304.8 34.3 %copy-start.7 = (bf16[512,1,1024]{2,0,1:T(8,128)(2,1)S(1)}, bf16[512,1,1024]{2,0,1:T(8,128)(2,1)}, u32[]{:S(2)}) copy-start(bf16[512,1,1024]{2,0,1:T(8,128)(2,1)} %reduce-scatter.5.cloned.1.call-done) | copy-start | bytes 3145732
  304.8 124.7 %all-gather.11.cloned.1.call-start = ((), (), s32[]{:S(2)}) async-start(), calls=%async_computation.14 | async-start | bytes 5242880 | tf_op jit(solution)/shard_map/all_gather | solution.py:278
  386.0 4.6 copy-start.11
  394.9 561.5 %all-reduce.5.cloned.1.call-start = ((), (), s32[]{:S(2)}) async-start(), calls=%async_computation.16 | async-start | bytes 12582912 | tf_op jit(solution)/shard_map/psum | solution.py:340
  395.0 9.5 copy-start.57
  395.0 9.5 copy-start.63
  404.5 25.1 %copy-start.61 = (bf16[256,1024]{1,0:T(8,128)(2,1)S(1)}, bf16[256,1024]{1,0:T(8,128)(2,1)}, u32[]{:S(2)}) copy-start(bf16[256,1024]{1,0:T(8,128)(2,1)} %param.26) | copy-start | bytes 1572868
  433.0 6.9 copy-start.9
  444.9 6.8 copy-start.2
  514.1 8.1 copy-start.2
  585.1 8.1 copy-start.2
  656.1 8.1 copy-start.2
  732.6 4.4 copy-start.19
  732.6 4.4 copy-start.22
  732.6 4.4 copy-start.24
  732.7 4.4 copy-start.56
  741.8 260.6 %reduce-scatter.11.cloned.1.call-start = ((), (), s32[]{:S(2)}) async-start(), calls=%async_computation.15 | async-start | bytes 5242880 | tf_op jit(solution)/shard_map/reduce_scatter | solution.py:315
  758.1 8.6 copy-start.5
  762.3 20.0 %all-to-all-start.3 = ((bf16[8,2,32768]{2,1,0:T(2,128)(2,1)}), bf16[8,2,32768]{2,1,0:T(2,128)(2,1)}, u32[]{:S(2)}, u32[]{:S(2)}) async-start(bf16[8,2,32768]{2,1,0:T(2,128)(2,1)} %reshape.985), calls=%async_computation.7 | async-start | bytes 2097152 | tf_op jit(solution)/shard_map/all_to_all | solution.py:242
  770.7 16.0 %copy-start.14 = (bf16[512,1,1024]{2,0,1:T(8,128)(2,1)S(1)}, bf16[512,1,1024]{2,0,1:T(8,128)(2,1)}, u32[]{:S(2)}) copy-start(bf16[512,1,1024]{2,0,1:T(8,128)(2,1)} %get-tuple-element.365) | copy-start | bytes 3145732
  782.4 22.3 %all-to-all-start.1 = ((bf16[8,2,32768]{2,1,0:T(2,128)(2,1)}), bf16[8,2,32768]{2,1,0:T(2,128)(2,1)}, u32[]{:S(2)}, u32[]{:S(2)}) async-start(bf16[8,2,32768]{2,1,0:T(2,128)(2,1)} %reshape.983), calls=%async_computation.3 | async-start | bytes 2097152 | tf_op jit(solution)/shard_map/all_to_all | solution.py:220
  790.5 17.9 %copy-start.31 = (s32[2,2048]{1,0:T(2,128)S(1)}, s32[2,2048]{1,0:T(2,128)}, u32[]{:S(2)}) copy-start(s32[2,2048]{1,0:T(2,128)} %get-tuple-element.373) | copy-start | bytes 49156
  804.7 31.1 %all-to-all-start = ((bf16[8,2,32768]{2,1,0:T(2,128)(2,1)}), bf16[8,2,32768]{2,1,0:T(2,128)(2,1)S(1)}, u32[]{:S(2)}, u32[]{:S(2)}) async-start(bf16[8,2,32768]{2,1,0:T(2,128)(2,1)} %reshape.981), calls=%async_computation.2 | async-start | bytes 2097152 | tf_op jit(solution)/shard_map/all_to_all | solution.py:219
  956.4 5.6 copy-start.18
  964.5 37.9 %copy-start.26 = (f32[1024]{0:T(1024)S(1)}, f32[1024]{0:T(1024)}, u32[]{:S(2)}) copy-start(f32[1024]{0:T(1024)} %copy-done.25) | copy-start | bytes 12292
  964.5 37.9 %copy-start.30 = (f32[512]{0:T(512)S(1)}, f32[512]{0:T(512)}, u32[]{:S(2)}) copy-start(f32[512]{0:T(512)} %copy-done.29) | copy-start | bytes 6148
  964.5 39.7 %copy-start.39 = (f32[512]{0:T(512)S(1)}, f32[512]{0:T(512)}, u32[]{:S(2)}) copy-start(f32[512]{0:T(512)} %copy-done.38) | copy-start | bytes 6148
  964.5 41.1 %copy-start.37 = (f32[512]{0:T(512)S(1)}, f32[512]{0:T(512)}, u32[]{:S(2)}) copy-start(f32[512]{0:T(512)} %copy-done.36) | copy-start | bytes 6148
  967.4 40.6 %copy-start.44 = (bf16[1024]{0:T(1024)(128)(2,1)S(1)}, bf16[1024]{0:T(1024)(128)(2,1)}, u32[]{:S(2)}) copy-start(bf16[1024]{0:T(1024)(128)(2,1)} %get-tuple-element.288) | copy-start | bytes 6148
  967.4 40.6 %copy-start.45 = (bf16[1024]{0:T(1024)(128)(2,1)S(1)}, bf16[1024]{0:T(1024)(128)(2,1)}, u32[]{:S(2)}) copy-start(bf16[1024]{0:T(1024)(128)(2,1)} %get-tuple-element.352) | copy-start | bytes 6148
  967.4 40.6 %copy-start.46 = (bf16[1024]{0:T(1024)(128)(2,1)S(1)}, bf16[1024]{0:T(1024)(128)(2,1)}, u32[]{:S(2)}) copy-start(bf16[1024]{0:T(1024)(128)(2,1)} %get-tuple-element.354) | copy-start | bytes 6148
  967.4 40.6 %copy-start.47 = (bf16[1024]{0:T(1024)(128)(2,1)S(1)}, bf16[1024]{0:T(1024)(128)(2,1)}, u32[]{:S(2)}) copy-start(bf16[1024]{0:T(1024)(128)(2,1)} %get-tuple-element.366) | copy-start | bytes 6148
  967.4 40.6 %copy-start.55 = (bf16[1024]{0:T(1024)(128)(2,1)S(1)}, bf16[1024]{0:T(1024)(128)(2,1)}, u32[]{:S(2)}) copy-start(bf16[1024]{0:T(1024)(128)(2,1)} %get-tuple-element.370) | copy-start | bytes 6148
  1046.2 18.2 %copy-start.1 = (bf16[1024,1024]{1,0:T(8,128)(2,1)S(1)}, bf16[1024,1024]{1,0:T(8,128)(2,1)}, u32[]{:S(2)}) copy-start(bf16[1024,1024]{1,0:T(8,128)(2,1)} %param.28) | copy-start | bytes 6291460
  (28 other events, 65.3 us)
Sparse Core Ops, SparseCore 0:
  15.2 37.1 all-gather.4
  139.6 44.4 reduce-scatter.4
  190.1 45.7 all-gather.6
  238.3 34.1 all-gather.8
  294.6 44.5 reduce-scatter.8
  341.5 44.4 reduce-scatter.6
  395.0 34.4 all-gather.10
  741.9 214.4 all-reduce.4
  958.9 43.4 reduce-scatter.10
